TPU v7x, 32 devices: a whole 2x2x4 slice. The times are simulated.
32 devices in a mesh: sub: 8 (over z, y), sec: 4 (over x, core).
Axes of the slice: x: 2, y: 2, z: 4, core: 2. Of those that a mesh axis runs over, the one named last changes fastest.
Arguments:
- start_vectors: bfloat16 [32, 3, 256, 512], P(None, None, 'sub', 'sec'), may hold values from -6 to 6
- stiffness: bfloat16 [3, 256, 512], P(None, 'sub', 'sec'), may hold values from 1.5 to 15
- coupling: bfloat16 [256, 512], P('sub', 'sec'), may hold values from -0.5 to 0.5
- kept_ranks: int32 [8, 4], P('sub', 'sec'), may hold values from 16 to 32, as said below
- level_start: float32 [256, 16], P('sub'), may hold values from -6 to 6
Outputs:
- prolonged: float32 [16, 3, 256, 512], P(None, None, 'sub', 'sec')
Inputs may be any that keep to these rules, and one draw needn't show every extreme that they name: `kept_ranks`: every subdomain keeps at least half of its 32 vectors; some subdomain keeps all 32 and some keeps exactly half.
All inputs are finite; a program needn't handle non-finite values.
Results may differ from a plain program's by a relative error of at most 0.0003.
Values may be sent and summed in bfloat16 or wider, within the bound.
No kernel may reach another device: no remote copies, remote signals or barrier semaphores. Data moves between devices by JAX's collectives and lax.ppermute only.
A program may use at most 64 MiB of HBM per device.

v0:
```python
import math
import jax
import jax.numpy as jnp
from jax import lax
from jax.sharding import PartitionSpec as P

CX = 32
H = 4
CY = 128
NV = 32
ITERS = 2
LEVEL_ITERS = 2
XEXT = 40
YEXT = 136
highest = lax.Precision.HIGHEST


def with_halo(x, sides, width):
    for axis, dim in sides:
        devices, length = (lax.axis_size(axis), x.shape[dim])
        up = [(i, (i + 1) % devices) for i in range(devices - 1)]
        down = [(j, i) for i, j in up]
        last = lax.slice_in_dim(x, length - width, length, axis=dim)
        leading = lax.slice_in_dim(x, 0, width, axis=dim)
        before = lax.ppermute(last, axis, up)
        after = lax.ppermute(leading, axis, down)
        x = jnp.concatenate([before, x, after], axis=dim)
    return x


def from_behind(block, axis, distance):
    devices = range(lax.axis_size(axis))
    route = [(i - distance, i) for i in devices if i - distance in devices]
    return lax.ppermute(block, axis, route)


def apply_operator(vectors, stiff_diag, shear_term, inside):
    padded = jnp.pad(vectors, ((0, 0), (0, 0), (1, 1), (1, 1)))
    beside = (
        padded[:, :, 2:, 1:-1]
        + padded[:, :, :-2, 1:-1]
        + padded[:, :, 1:-1, 2:]
        + padded[:, :, 1:-1, :-2]
    )
    others = jnp.sum(vectors, axis=1, keepdims=True) - vectors
    return ((4.0 + stiff_diag) * vectors - beside + shear_term * others) * inside


def orthonormal(work):
    shape_before = work.shape
    flat = work.reshape(shape_before[0], -1)
    gram = jnp.dot(flat, flat.T, precision=highest)
    lower = jnp.linalg.cholesky(gram)
    solved = lax.linalg.triangular_solve(lower, flat, left_side=True, lower=True)
    return solved.reshape(shape_before)


def subspace_basis(vectors, stiff_diag, shear_term, inside, rank):
    for iteration in range(ITERS):
        vectors = orthonormal(apply_operator(vectors, stiff_diag, shear_term, inside))
    live = (jnp.arange(NV, dtype=jnp.int32) < rank).astype(jnp.float32)
    basis = vectors * live[:, None, None, None]
    image = apply_operator(basis, stiff_diag, shear_term, inside)
    self_block = jnp.dot(basis.reshape(NV, -1), image.reshape(NV, -1).T, precision=highest)
    return (basis, self_block)


def on_device(start_vectors, stiffness, coupling, kept_ranks, level_start):
    span_count = lax.axis_size("sub")
    sect_count = lax.axis_size("sec")
    stacked = jnp.concatenate(
        [start_vectors.reshape(NV * 3, CX, CY), stiffness, coupling[None]], axis=0
    )
    extended = with_halo(stacked, (("sub", 1), ("sec", 2)), H)
    vectors = extended[: NV * 3].astype(jnp.float32).reshape(NV, 3, XEXT, YEXT)
    stiff_diag = extended[NV * 3 : NV * 3 + 3].astype(jnp.float32)
    shear_term = extended[NV * 3 + 3].astype(jnp.float32)
    row_global = lax.axis_index("sub") * CX - H + lax.iota(jnp.int32, XEXT)
    col_global = lax.axis_index("sec") * CY - H + lax.iota(jnp.int32, YEXT)
    row_inside = (row_global >= 0) & (row_global < span_count * CX)
    col_inside = (col_global >= 0) & (col_global < sect_count * CY)
    inside = (row_inside[:, None] & col_inside[None, :]).astype(jnp.float32)
    basis, self_block = subspace_basis(vectors, stiff_diag, shear_term, inside, kept_ranks[0, 0])
    lower_next = from_behind(basis[:, :, : 2 * H, :], "sub", -1)
    upper_rim = (4.0 + stiff_diag[:, CX:, :]) * basis[:, :, CX:, :]
    couple_block = jnp.einsum("acxy,bcxy->ab", upper_rim, lower_next, precision=highest)
    own_rows = level_start
    couple_prev = from_behind(couple_block, "sub", 1)
    for iteration in range(LEVEL_ITERS):
        rows_next = from_behind(own_rows, "sub", -1)
        image = jnp.dot(self_block, own_rows, precision=highest)
        image = image + jnp.dot(couple_block, rows_next, precision=highest)
        rows_prev = from_behind(own_rows, "sub", 1)
        image = image + jnp.dot(couple_prev.T, rows_prev, precision=highest)
        gram = lax.psum(jnp.dot(image.T, image, precision=highest), "sub")
        lower = jnp.linalg.cholesky(gram)
        own_rows = lax.linalg.triangular_solve(lower, image.T, left_side=True, lower=True).T
    factor = math.sqrt(span_count * 3 * XEXT * YEXT)
    owned = basis[:, :, H : H + CX, H : H + CY]
    return factor * jnp.einsum("ak,acxy->kcxy", own_rows, owned, precision=highest)


def solution(mesh):
    placed = (
        P(None, None, "sub", "sec"),
        P(None, "sub", "sec"),
        P("sub", "sec"),
        P("sub", "sec"),
        P("sub", None),
    )
    return jax.shard_map(
        on_device,
        mesh=mesh,
        in_specs=placed,
        out_specs=P(None, None, "sub", "sec"),
        check_vma=False,
    )
```

profile of v0, /device:TPU:0, one launch (start us, length us, event | category | flops | bytes accessed | tf_op | source)
XLA Modules:
  0.0 206.8 jit_solution(7046180540235981564)
XLA Ops:
  0.0 4.9 %collective-permute-start.7 = (f32[32,16]{0,1:T(8,128)}, f32[32,16]{0,1:T(8,128)S(1)}, u32[]{:S(2)}, u32[]{:S(2)}) collective-permute-start(f32[32,16]{0,1:T(8,128)} %param.15), channel_id=1, source_target_pairs={{0,4},{4,8},{8,12},{12,16},{16,20},{20,24},{24,28},{1,5},{5,9},{9,... | collective-permute-start | bytes 6152 | tf_op jit(solution)/shard_map/ppermute | solution.py:34
  7.4 4.6 %collective-permute-start = (bf16[100,4,128]{2,1,0:T(4,128)(2,1)S(1)}, bf16[100,4,128]{2,1,0:T(4,128)(2,1)S(1)}, u32[]{:S(2)}, u32[]{:S(2)}) collective-permute-start(bf16[100,4,128]{2,1,0:T(4,128)(2,1)S(1)} %get-tuple-element.15), channel_id=1, source_target_pairs={{0,4},{4,8},{8,12},{12,16},{16,20},{20,24},{24,28},{1,5},{5,9},{9,... | collective-permute-start | bytes 307208 | tf_op jit(solution)/shard_map/ppermute | solution.py:25
  14.2 4.7 %collective-permute-done.1 = bf16[100,4,128]{2,1,0:T(4,128)(2,1)S(1)} collective-permute-done((bf16[100,4,128]{2,1,0:T(4,128)(2,1)S(1)}, bf16[100,4,128]{2,1,0:T(4,128)(2,1)S(1)}, u32[]{:S(2)}, u32[]{:S(2)}) %collective-permute-start.1) | collective-permute-done | bytes 102432 | tf_op jit(solution)/shard_map/ppermute | solution.py:26
  28.9 4.9 %pad_maximum_fusion = bf16[100,40,136]{2,1,0:T(8,128)(2,1)S(1)} fusion(bf16[100,40,4]{2,1,0:T(8,128)(2,1)S(1)} %copy.36, bf16[100,4,128]{2,1,0:T(4,128)(2,1)S(1)} %collective-permute-done.1, bf16[1,32,128]{2,1,0:T(8,128)(2,1)S(1)} %bitcast.112, bf16[3,32,128]{2,1,0:T(8,128)(2,1)S(1)} %copy-done.2, bf16[96,32,128]{2,1,0:T(8,128)(2,1)S(1)} %bitcast.105, ...), kind=kLoop, calls=%fused_computation.24 | loop fusion | flops 7616000 | bytes 2176000 | tf_op jit(solution)/shard_map/concatenate | solution.py:27
  38.4 3.2 %convolution_bitcast_fusion.2 = f32[32,32]{1,0:T(8,128)S(1)} fusion(f32[32,3,40,136]{3,0,2,1:T(8,128)S(1)} %add_multiply_fusion.1), kind=kOutput, calls=%fused_computation.35 | convolution fusion | flops 200540160 | bytes 2093056 | tf_op jit(solution)/shard_map/dot_general | solution.py:52
  41.6 4.2 %copy.42 = f32[32,3,40,136]{3,2,1,0:T(8,128)} copy(f32[32,3,40,136]{3,0,2,1:T(8,128)S(1)} %add_multiply_fusion.1) | data formatting | bytes 4177920 | tf_op jit(solution)/shard_map/mul | solution.py:46
  45.8 3.6 %reshape.107 = f32[32,16320]{1,0:T(8,128)S(1)} reshape(f32[32,3,40,136]{3,2,1,0:T(8,128)} %copy.42) | data formatting | bytes 4177920 | tf_op jit(solution)/shard_map/reshape | solution.py:51
  56.2 3.3 %fusion.35 = f32[32,16320]{1,0:T(8,128)} fusion(f32[32,16320]{1,0:T(8,128)S(1)} %reshape.107, f32[1,32,32]{1,2,0:T(8,128)S(1)} %custom-call.12), kind=kOutput, calls=%fused_computation.62 | convolution fusion | flops 200540160 | bytes 4182016 | tf_op jit(solution)/shard_map/triangular_solve/dot.1 | solution.py:54
  59.4 5.0 %reshape.108 = f32[32,3,40,136]{3,2,1,0:T(8,128)} reshape(f32[32,16320]{1,0:T(8,128)} %fusion.35) | data formatting | bytes 4177920 | tf_op jit(solution)/shard_map/reshape | solution.py:55
  64.5 5.2 %copy.43 = f32[32,3,40,136]{3,0,2,1:T(8,128)} copy(f32[32,3,40,136]{3,2,1,0:T(8,128)} %reshape.108) | data formatting | bytes 4177920 | tf_op jit(solution)/shard_map/reshape | solution.py:55
  72.7 9.0 %add_multiply_fusion = f32[32,3,40,136]{3,0,2,1:T(8,128)S(1)} fusion(f32[32,3,40,136]{3,0,2,1:T(8,128)} %copy.43, f32[32,40,136]{2,0,1:T(8,128)S(1)} %copy.45, f32[40,136]{1,0:T(8,128)S(1)} %and_convert_fusion, f32[40,136]{1,0:T(8,128)S(1)} %fusion.29, f32[3,40,136]{2,1,0:T(8,128)S(1)} %get-tuple-element.10), kind=kLoop, calls=%fused_computation.16 | loop fusion | flops 4700160 | bytes 4983040 | tf_op jit(solution)/shard_map/mul | solution.py:46
  81.7 3.2 %convolution_bitcast_fusion.1 = f32[32,32]{1,0:T(8,128)S(1)} fusion(f32[32,3,40,136]{3,0,2,1:T(8,128)S(1)} %add_multiply_fusion), kind=kOutput, calls=%fused_computation.34 | convolution fusion | flops 200540160 | bytes 2093056 | tf_op jit(solution)/shard_map/dot_general | solution.py:52
  84.9 4.2 %copy.48 = f32[32,3,40,136]{3,2,1,0:T(8,128)} copy(f32[32,3,40,136]{3,0,2,1:T(8,128)S(1)} %add_multiply_fusion) | data formatting | bytes 4177920 | tf_op jit(solution)/shard_map/mul | solution.py:46
  89.0 3.1 %reshape.109 = f32[32,16320]{1,0:T(8,128)S(1)} reshape(f32[32,3,40,136]{3,2,1,0:T(8,128)} %copy.48) | data formatting | bytes 4177920 | tf_op jit(solution)/shard_map/reshape | solution.py:51
  98.9 3.3 %fusion.32 = f32[32,16320]{1,0:T(8,128)} fusion(f32[32,16320]{1,0:T(8,128)S(1)} %reshape.109, f32[1,32,32]{1,2,0:T(8,128)S(1)} %custom-call.13), kind=kOutput, calls=%fused_computation.58 | convolution fusion | flops 200540160 | bytes 4182016 | tf_op jit(solution)/shard_map/triangular_solve/dot.1 | solution.py:54
  102.2 5.2 %reshape.110 = f32[32,3,40,136]{3,2,1,0:T(8,128)} reshape(f32[32,16320]{1,0:T(8,128)} %fusion.32) | data formatting | bytes 4177920 | tf_op jit(solution)/shard_map/reshape | solution.py:55
  107.4 3.9 %fusion.52 = (f32[32,40,136]{2,0,1:T(8,128)S(1)}, f32[32,3,40,136]{3,0,2,1:T(8,128)S(1)}) fusion(f32[32]{0:T(128)S(1)} %compare_convert_fusion, f32[32,3,40,136]{3,2,1,0:T(8,128)} %reshape.110), kind=kLoop, calls=%fused_computation.97 | loop fusion | flops 870400 | bytes 4874368 | tf_op jit(solution)/shard_map/reduce_sum | solution.py:45
  111.4 5.0 %fusion.25 = f32[32,32]{1,0:T(8,128)S(1)} fusion(f32[32,3,40,136]{3,0,2,1:T(8,128)S(1)} %get-tuple-element.8, f32[32,40,136]{2,0,1:T(8,128)S(1)} %get-tuple-element.6, f32[40,136]{1,0:T(8,128)S(1)} %and_convert_fusion, f32[40,136]{1,0:T(8,128)S(1)} %fusion.29, f32[3,40,136]{2,1,0:T(8,128)S(1)} %get-tuple-element.10), kind=kOutput, calls=%fused_computation.33 | convolution fusion | flops 205240320 | bytes 9383936 | tf_op jit(solution)/shard_map/dot_general | solution.py:64
  117.9 21.1 %collective-permute-done.4 = f32[32,3,8,136]{3,0,2,1:T(8,128)S(1)} collective-permute-done((f32[32,3,8,136]{3,0,2,1:T(8,128)S(1)}, f32[32,3,8,136]{3,0,2,1:T(8,128)S(1)}, u32[]{:S(2)}, u32[]{:S(2)}) %collective-permute-start.4) | collective-permute-done | bytes 417824 | tf_op jit(solution)/shard_map/ppermute | solution.py:34
  139.8 5.1 %collective-permute-start.6 = (f32[32,32]{1,0:T(8,128)S(1)}, f32[32,32]{1,0:T(8,128)S(1)}, u32[]{:S(2)}, u32[]{:S(2)}) collective-permute-start(f32[32,32]{1,0:T(8,128)S(1)} %convolution_bitcast_fusion), channel_id=1, source_target_pairs={{0,4},{4,8},{8,12},{12,16},{16,20},{20,24},{24,28},{1,5},{5,9},{9,... | collective-permute-start | bytes 12296 | tf_op jit(solution)/shard_map/ppermute | solution.py:34
  146.6 20.0 %psum.14 = f32[16,16]{0,1:T(8,128)S(1)} all-reduce(f32[16,16]{0,1:T(8,128)S(1)} %fusion.55), channel_id=1, replica_groups=mesh['sub'=8,'sec'=4] {'sub'}, use_global_device_ids=true, to_apply=%region_5.8 | all-reduce | flops 256 | bytes 2048 | tf_op jit(solution)/shard_map/psum | solution.py:95
  172.3 4.6 %collective-permute-start.9 = (f32[32,16]{0,1:T(8,128)S(1)}, f32[32,16]{0,1:T(8,128)S(1)}, u32[]{:S(2)}, u32[]{:S(2)}) collective-permute-start(f32[32,16]{0,1:T(8,128)S(1)} %bitcast.116), channel_id=1, source_target_pairs={{0,4},{4,8},{8,12},{12,16},{16,20},{20,24},{24,28},{1,5},{5,9},{9,... | collective-permute-start | bytes 6152 | tf_op jit(solution)/shard_map/ppermute | solution.py:34
  178.5 19.7 %psum.15 = f32[16,16]{0,1:T(8,128)S(1)} all-reduce(f32[16,16]{0,1:T(8,128)S(1)} %fusion.57), channel_id=1, replica_groups=mesh['sub'=8,'sec'=4] {'sub'}, use_global_device_ids=true, to_apply=%region_8.13 | all-reduce | flops 256 | bytes 2048 | tf_op jit(solution)/shard_map/psum | solution.py:95
  202.4 3.0 %fusion.22 = f32[16,3,32,128]{3,0,2,1:T(8,128)S(1)} fusion(f32[16,32,1,1]{1,0,3,2:T(8,128)S(1)} %convolution_bitcast_fusion.3, f32[32,3,40,136]{3,0,2,1:T(8,128)} %copy-done.1), kind=kOutput, calls=%fused_computation.31 | convolution fusion | flops 75694080 | bytes 2361344 | tf_op jit(solution)/shard_map/ak,acxy->kcxy/dot_general | solution.py:100
  (86 shorter events, 51.8 us)
Async XLA Ops:
  0.0 145.0 %collective-permute-start.7 = (f32[32,16]{0,1:T(8,128)}, f32[32,16]{0,1:T(8,128)S(1)}, u32[]{:S(2)}, u32[]{:S(2)}) collective-permute-start(f32[32,16]{0,1:T(8,128)} %param.15), channel_id=1, source_target_pairs={{0,4},{4,8},{8,12},{12,16},{16,20},{20,24},{24,28},{1,5},{5,9},{9,... | collective-permute-start | bytes 6152 | tf_op jit(solution)/shard_map/ppermute | solution.py:34
  4.9 140.0 %collective-permute-start.5 = (f32[32,16]{0,1:T(8,128)}, f32[32,16]{0,1:T(8,128)S(1)}, u32[]{:S(2)}, u32[]{:S(2)}) collective-permute-start(f32[32,16]{0,1:T(8,128)} %param.15), channel_id=1, source_target_pairs={{4,0},{8,4},{12,8},{16,12},{20,16},{24,20},{28,24},{5,1},{9,5},{13... | collective-permute-start | bytes 6152 | tf_op jit(solution)/shard_map/ppermute | solution.py:34
  7.4 6.8 %collective-permute-start = (bf16[100,4,128]{2,1,0:T(4,128)(2,1)S(1)}, bf16[100,4,128]{2,1,0:T(4,128)(2,1)S(1)}, u32[]{:S(2)}, u32[]{:S(2)}) collective-permute-start(bf16[100,4,128]{2,1,0:T(4,128)(2,1)S(1)} %get-tuple-element.15), channel_id=1, source_target_pairs={{0,4},{4,8},{8,12},{12,16},{16,20},{20,24},{24,28},{1,5},{5,9},{9,... | collective-permute-start | bytes 307208 | tf_op jit(solution)/shard_map/ppermute | solution.py:25
  11.9 7.0 %collective-permute-start.1 = (bf16[100,4,128]{2,1,0:T(4,128)(2,1)S(1)}, bf16[100,4,128]{2,1,0:T(4,128)(2,1)S(1)}, u32[]{:S(2)}, u32[]{:S(2)}) collective-permute-start(bf16[100,4,128]{2,1,0:T(4,128)(2,1)S(1)} %get-tuple-element.16), channel_id=1, source_target_pairs={{4,0},{8,4},{12,8},{16,12},{20,16},{24,20},{28,24},{5,1},{9,5},{13... | collective-permute-start | bytes 307208 | tf_op jit(solution)/shard_map/ppermute | solution.py:26
  20.6 8.2 %copy-start = (bf16[32,3,32,128]{3,2,1,0:T(8,128)(2,1)S(1)}, bf16[32,3,32,128]{3,2,1,0:T(8,128)(2,1)}, u32[]{:S(2)}) copy-start(bf16[32,3,32,128]{3,2,1,0:T(8,128)(2,1)} %param.11) | copy-start | bytes 2359300
  20.6 8.2 %copy-start.2 = (bf16[3,32,128]{2,1,0:T(8,128)(2,1)S(1)}, bf16[3,32,128]{2,1,0:T(8,128)(2,1)}, u32[]{:S(2)}) copy-start(bf16[3,32,128]{2,1,0:T(8,128)(2,1)} %param.12) | copy-start | bytes 73732
  20.6 8.2 %copy-start.3 = (bf16[32,128]{1,0:T(8,128)(2,1)S(1)}, bf16[32,128]{1,0:T(8,128)(2,1)}, u32[]{:S(2)}) copy-start(bf16[32,128]{1,0:T(8,128)(2,1)} %param.13) | copy-start | bytes 24580
  22.4 5.8 %collective-permute-start.3 = (bf16[100,40,4]{0,1,2:T(8,128)(2,1)S(1)}, bf16[100,40,4]{0,1,2:T(8,128)(2,1)S(1)}, u32[]{:S(2)}, u32[]{:S(2)}) collective-permute-start(bf16[100,40,4]{0,1,2:T(8,128)(2,1)S(1)} %copy.34), channel_id=1, source_target_pairs={{1,0},{2,1},{3,2},{5,4},{6,5},{7,6},{9,8},{10,9},{11,10},{13,12},{... | collective-permute-start | bytes 96008 | tf_op jit(solution)/shard_map/ppermute | solution.py:26
  23.7 3.9 %collective-permute-start.2 = (bf16[100,40,4]{0,1,2:T(8,128)(2,1)S(1)}, bf16[100,40,4]{0,1,2:T(8,128)(2,1)S(1)}, u32[]{:S(2)}, u32[]{:S(2)}) collective-permute-start(bf16[100,40,4]{0,1,2:T(8,128)(2,1)S(1)} %copy.33), channel_id=1, source_target_pairs={{0,1},{1,2},{2,3},{4,5},{5,6},{6,7},{8,9},{9,10},{10,11},{12,13},{... | collective-permute-start | bytes 96008 | tf_op jit(solution)/shard_map/ppermute | solution.py:25
  111.3 27.6 %copy-start.1 = (f32[32,3,40,136]{3,0,2,1:T(8,128)}, f32[32,3,40,136]{3,0,2,1:T(8,128)S(1)}, u32[]{:S(2)}) copy-start(f32[32,3,40,136]{3,0,2,1:T(8,128)S(1)} %get-tuple-element.8) | copy-start | bytes 6266884
  111.4 6.3 %copy-start.4 = (f32[32,16]{0,1:T(8,128)S(1)}, f32[32,16]{0,1:T(8,128)}, u32[]{:S(2)}) copy-start(f32[32,16]{0,1:T(8,128)} %param.15) | copy-start | bytes 6148
  116.4 22.6 %collective-permute-start.4 = (f32[32,3,8,136]{3,0,2,1:T(8,128)S(1)}, f32[32,3,8,136]{3,0,2,1:T(8,128)S(1)}, u32[]{:S(2)}, u32[]{:S(2)}) collective-permute-start(f32[32,3,8,136]{3,0,2,1:T(8,128)S(1)} %slice.109), channel_id=1, source_target_pairs={{4,0},{8,4},{12,8},{16,12},{20,16},{24,20},{28,24},{5,1},{9,5},{13... | collective-permute-start | bytes 1253384 | tf_op jit(solution)/shard_map/ppermute | solution.py:34
  139.8 6.5 %collective-permute-start.6 = (f32[32,32]{1,0:T(8,128)S(1)}, f32[32,32]{1,0:T(8,128)S(1)}, u32[]{:S(2)}, u32[]{:S(2)}) collective-permute-start(f32[32,32]{1,0:T(8,128)S(1)} %convolution_bitcast_fusion), channel_id=1, source_target_pairs={{0,4},{4,8},{8,12},{12,16},{16,20},{20,24},{24,28},{1,5},{5,9},{9,... | collective-permute-start | bytes 12296 | tf_op jit(solution)/shard_map/ppermute | solution.py:34
  170.8 6.0 %collective-permute-start.8 = (f32[32,16]{0,1:T(8,128)S(1)}, f32[32,16]{0,1:T(8,128)S(1)}, u32[]{:S(2)}, u32[]{:S(2)}) collective-permute-start(f32[32,16]{0,1:T(8,128)S(1)} %bitcast.115), channel_id=1, source_target_pairs={{4,0},{8,4},{12,8},{16,12},{20,16},{24,20},{28,24},{5,1},{9,5},{13... | collective-permute-start | bytes 6152 | tf_op jit(solution)/shard_map/ppermute | solution.py:34
  172.3 5.9 %collective-permute-start.9 = (f32[32,16]{0,1:T(8,128)S(1)}, f32[32,16]{0,1:T(8,128)S(1)}, u32[]{:S(2)}, u32[]{:S(2)}) collective-permute-start(f32[32,16]{0,1:T(8,128)S(1)} %bitcast.116), channel_id=1, source_target_pairs={{0,4},{4,8},{8,12},{12,16},{16,20},{20,24},{24,28},{1,5},{5,9},{9,... | collective-permute-start | bytes 6152 | tf_op jit(solution)/shard_map/ppermute | solution.py:34
where the time goes:
time: 211 us; the launch traced here: 207 us
  other arithmetic  48.2 us (23%)
  blocking collectives  39.6 us (19%)
  local copies, waits for them, and re-layouts  36.5 us (17%)
  waiting for transfers between devices  29.3 us (14%)
  starting transfers between devices  28.6 us (14%)
  matrix products  23.2 us (11%)
    psum x2, blocking collectives, on_device(): gram = lax.psum(jnp.dot(image.T, image, precision=highest), 'sub')  39.6 us
    ppermute x6, waiting for transfers between devices, from_behind(): return lax.ppermute(block, axis, route)  23.6 us
    ppermute x6, starting transfers between devices, from_behind(): return lax.ppermute(block, axis, route)  18.4 us
    reshape x3, local copies, waits for them, and re-layouts, orthonormal(): return solved.reshape(shape_before)  15.5 us
    mul x2, other arithmetic, apply_operator(): ((4.0 + stiff_diag) * vectors - beside + shear_term * others) * inside  12 us
    mul x2, local copies, waits for them, and re-layouts, apply_operator(): ((4.0 + stiff_diag) * vectors - beside + shear_term * others) * inside  8.31 us
    ppermute x2, starting transfers between devices, with_halo(): before = lax.ppermute(last, axis, up)  7.59 us
    another operation x6, other arithmetic, orthonormal(): lower = jnp.linalg.cholesky(gram)  7.19 us
  transfers between devices with their start and end apart: 10, of which 6 were waited for; matrix products, arithmetic and copies ran while one was open for 46% of the time, Pallas kernels for 0%

commit v1 on v0

--- a/solution.py
+++ b/solution.py
@@ -92,7 +92,7 @@
         image = image + jnp.dot(couple_block, rows_next, precision=highest)
         rows_prev = from_behind(own_rows, "sub", 1)
         image = image + jnp.dot(couple_prev.T, rows_prev, precision=highest)
-        gram = lax.psum(jnp.dot(image.T, image, precision=highest), "sub")
+        gram = jnp.sum(lax.all_gather(jnp.dot(image.T, image, precision=highest), "sub"), axis=0)
         lower = jnp.linalg.cholesky(gram)
         own_rows = lax.linalg.triangular_solve(lower, image.T, left_side=True, lower=True).T
     factor = math.sqrt(span_count * 3 * XEXT * YEXT)

time: 211 us -> 233 us (1.10)
  blocking collectives: 39.6 us -> 61.6 us
    all_gather x0 -> x2, blocking collectives: none -> 61.6 us  [on_device(): lax.all_gather(jnp.dot(image.T, image, precision=highest), 'sub')]
    psum x2 -> x0, blocking collectives: 39.6 us -> none  [on_device(): gram = lax.psum(jnp.dot(image.T, image, precision=highest), 'sub')]
  transfers between devices with their start and end apart: 10 -> 10, of which waited for: 6 -> 6; matrix products, arithmetic and copies ran while one was open for 46% -> 41% of each run, Pallas kernels for 0% -> 0%
where the time goes in v1:
time: 233 us; the launch traced here: 229 us
  blocking collectives  61.6 us (26%)
  other arithmetic  48.3 us (21%)
  local copies, waits for them, and re-layouts  36.5 us (16%)
  waiting for transfers between devices  29.3 us (13%)
  starting transfers between devices  28.6 us (12%)
  matrix products  23.2 us (10%)
    all_gather x2, blocking collectives, on_device(): lax.all_gather(jnp.dot(image.T, image, precision=highest), 'sub')  61.6 us
    ppermute x6, waiting for transfers between devices, from_behind(): return lax.ppermute(block, axis, route)  23.6 us
    ppermute x6, starting transfers between devices, from_behind(): return lax.ppermute(block, axis, route)  18.4 us
    reshape x3, local copies, waits for them, and re-layouts, orthonormal(): return solved.reshape(shape_before)  15.5 us
    mul x2, other arithmetic, apply_operator(): ((4.0 + stiff_diag) * vectors - beside + shear_term * others) * inside  12 us
    mul x2, local copies, waits for them, and re-layouts, apply_operator(): ((4.0 + stiff_diag) * vectors - beside + shear_term * others) * inside  8.31 us
    ppermute x2, starting transfers between devices, with_halo(): before = lax.ppermute(last, axis, up)  7.59 us
    another operation x6, other arithmetic, orthonormal(): lower = jnp.linalg.cholesky(gram)  7.19 us
  transfers between devices with their start and end apart: 10, of which 6 were waited for; matrix products, arithmetic and copies ran while one was open for 41% of the time, Pallas kernels for 0%

profile of v1, /device:TPU:0, one launch (start us, length us, event | category | flops | bytes accessed | tf_op | source)
XLA Modules:
  0.0 228.8 jit_solution(14026721271305486923)
XLA Ops:
  0.0 4.9 %collective-permute-start.7 = (f32[32,16]{0,1:T(8,128)}, f32[32,16]{0,1:T(8,128)S(1)}, u32[]{:S(2)}, u32[]{:S(2)}) collective-permute-start(f32[32,16]{0,1:T(8,128)} %param.15), channel_id=1, source_target_pairs={{0,4},{4,8},{8,12},{12,16},{16,20},{20,24},{24,28},{1,5},{5,9},{9,... | collective-permute-start | bytes 6152 | tf_op jit(solution)/shard_map/ppermute | solution.py:34
  7.4 4.6 %collective-permute-start = (bf16[100,4,128]{2,1,0:T(4,128)(2,1)S(1)}, bf16[100,4,128]{2,1,0:T(4,128)(2,1)S(1)}, u32[]{:S(2)}, u32[]{:S(2)}) collective-permute-start(bf16[100,4,128]{2,1,0:T(4,128)(2,1)S(1)} %get-tuple-element.15), channel_id=1, source_target_pairs={{0,4},{4,8},{8,12},{12,16},{16,20},{20,24},{24,28},{1,5},{5,9},{9,... | collective-permute-start | bytes 307208 | tf_op jit(solution)/shard_map/ppermute | solution.py:25
  14.2 4.7 %collective-permute-done.1 = bf16[100,4,128]{2,1,0:T(4,128)(2,1)S(1)} collective-permute-done((bf16[100,4,128]{2,1,0:T(4,128)(2,1)S(1)}, bf16[100,4,128]{2,1,0:T(4,128)(2,1)S(1)}, u32[]{:S(2)}, u32[]{:S(2)}) %collective-permute-start.1) | collective-permute-done | bytes 102432 | tf_op jit(solution)/shard_map/ppermute | solution.py:26
  28.9 4.9 %pad_maximum_fusion = bf16[100,40,136]{2,1,0:T(8,128)(2,1)S(1)} fusion(bf16[100,40,4]{2,1,0:T(8,128)(2,1)S(1)} %copy.32, bf16[100,4,128]{2,1,0:T(4,128)(2,1)S(1)} %collective-permute-done.1, bf16[1,32,128]{2,1,0:T(8,128)(2,1)S(1)} %bitcast.116, bf16[3,32,128]{2,1,0:T(8,128)(2,1)S(1)} %copy-done.2, bf16[96,32,128]{2,1,0:T(8,128)(2,1)S(1)} %bitcast.107, ...), kind=kLoop, calls=%fused_computation.24 | loop fusion | flops 7616000 | bytes 2176000 | tf_op jit(solution)/shard_map/concatenate | solution.py:27
  38.4 3.2 %convolution_bitcast_fusion.2 = f32[32,32]{1,0:T(8,128)S(1)} fusion(f32[32,3,40,136]{3,0,2,1:T(8,128)S(1)} %add_multiply_fusion.1), kind=kOutput, calls=%fused_computation.35 | convolution fusion | flops 200540160 | bytes 2093056 | tf_op jit(solution)/shard_map/dot_general | solution.py:52
  41.6 4.2 %copy.38 = f32[32,3,40,136]{3,2,1,0:T(8,128)} copy(f32[32,3,40,136]{3,0,2,1:T(8,128)S(1)} %add_multiply_fusion.1) | data formatting | bytes 4177920 | tf_op jit(solution)/shard_map/mul | solution.py:46
  45.8 3.6 %reshape.107 = f32[32,16320]{1,0:T(8,128)S(1)} reshape(f32[32,3,40,136]{3,2,1,0:T(8,128)} %copy.38) | data formatting | bytes 4177920 | tf_op jit(solution)/shard_map/reshape | solution.py:51
  56.2 3.3 %fusion.35 = f32[32,16320]{1,0:T(8,128)} fusion(f32[32,16320]{1,0:T(8,128)S(1)} %reshape.107, f32[1,32,32]{1,2,0:T(8,128)S(1)} %custom-call.12), kind=kOutput, calls=%fused_computation.62 | convolution fusion | flops 200540160 | bytes 4182016 | tf_op jit(solution)/shard_map/triangular_solve/dot.1 | solution.py:54
  59.4 5.0 %reshape.108 = f32[32,3,40,136]{3,2,1,0:T(8,128)} reshape(f32[32,16320]{1,0:T(8,128)} %fusion.35) | data formatting | bytes 4177920 | tf_op jit(solution)/shard_map/reshape | solution.py:55
  64.5 5.2 %copy.39 = f32[32,3,40,136]{3,0,2,1:T(8,128)} copy(f32[32,3,40,136]{3,2,1,0:T(8,128)} %reshape.108) | data formatting | bytes 4177920 | tf_op jit(solution)/shard_map/reshape | solution.py:55
  72.7 9.0 %add_multiply_fusion = f32[32,3,40,136]{3,0,2,1:T(8,128)S(1)} fusion(f32[32,3,40,136]{3,0,2,1:T(8,128)} %copy.39, f32[32,40,136]{2,0,1:T(8,128)S(1)} %copy.41, f32[40,136]{1,0:T(8,128)S(1)} %and_convert_fusion, f32[40,136]{1,0:T(8,128)S(1)} %fusion.29, f32[3,40,136]{2,1,0:T(8,128)S(1)} %get-tuple-element.10), kind=kLoop, calls=%fused_computation.16 | loop fusion | flops 4700160 | bytes 4983040 | tf_op jit(solution)/shard_map/mul | solution.py:46
  81.7 3.2 %convolution_bitcast_fusion.1 = f32[32,32]{1,0:T(8,128)S(1)} fusion(f32[32,3,40,136]{3,0,2,1:T(8,128)S(1)} %add_multiply_fusion), kind=kOutput, calls=%fused_computation.34 | convolution fusion | flops 200540160 | bytes 2093056 | tf_op jit(solution)/shard_map/dot_general | solution.py:52
  84.9 4.2 %copy.44 = f32[32,3,40,136]{3,2,1,0:T(8,128)} copy(f32[32,3,40,136]{3,0,2,1:T(8,128)S(1)} %add_multiply_fusion) | data formatting | bytes 4177920 | tf_op jit(solution)/shard_map/mul | solution.py:46
  89.0 3.1 %reshape.109 = f32[32,16320]{1,0:T(8,128)S(1)} reshape(f32[32,3,40,136]{3,2,1,0:T(8,128)} %copy.44) | data formatting | bytes 4177920 | tf_op jit(solution)/shard_map/reshape | solution.py:51
  98.9 3.3 %fusion.32 = f32[32,16320]{1,0:T(8,128)} fusion(f32[32,16320]{1,0:T(8,128)S(1)} %reshape.109, f32[1,32,32]{1,2,0:T(8,128)S(1)} %custom-call.13), kind=kOutput, calls=%fused_computation.58 | convolution fusion | flops 200540160 | bytes 4182016 | tf_op jit(solution)/shard_map/triangular_solve/dot.1 | solution.py:54
  102.2 5.2 %reshape.110 = f32[32,3,40,136]{3,2,1,0:T(8,128)} reshape(f32[32,16320]{1,0:T(8,128)} %fusion.32) | data formatting | bytes 4177920 | tf_op jit(solution)/shard_map/reshape | solution.py:55
  107.4 3.9 %fusion.52 = (f32[32,40,136]{2,0,1:T(8,128)S(1)}, f32[32,3,40,136]{3,0,2,1:T(8,128)S(1)}) fusion(f32[32]{0:T(128)S(1)} %compare_convert_fusion, f32[32,3,40,136]{3,2,1,0:T(8,128)} %reshape.110), kind=kLoop, calls=%fused_computation.97 | loop fusion | flops 870400 | bytes 4874368 | tf_op jit(solution)/shard_map/reduce_sum | solution.py:45
  111.4 5.0 %fusion.25 = f32[32,32]{1,0:T(8,128)S(1)} fusion(f32[32,3,40,136]{3,0,2,1:T(8,128)S(1)} %get-tuple-element.8, f32[32,40,136]{2,0,1:T(8,128)S(1)} %get-tuple-element.6, f32[40,136]{1,0:T(8,128)S(1)} %and_convert_fusion, f32[40,136]{1,0:T(8,128)S(1)} %fusion.29, f32[3,40,136]{2,1,0:T(8,128)S(1)} %get-tuple-element.10), kind=kOutput, calls=%fused_computation.33 | convolution fusion | flops 205240320 | bytes 9383936 | tf_op jit(solution)/shard_map/dot_general | solution.py:64
  117.9 21.1 %collective-permute-done.4 = f32[32,3,8,136]{3,0,2,1:T(8,128)S(1)} collective-permute-done((f32[32,3,8,136]{3,0,2,1:T(8,128)S(1)}, f32[32,3,8,136]{3,0,2,1:T(8,128)S(1)}, u32[]{:S(2)}, u32[]{:S(2)}) %collective-permute-start.4) | collective-permute-done | bytes 417824 | tf_op jit(solution)/shard_map/ppermute | solution.py:34
  139.8 5.1 %collective-permute-start.6 = (f32[32,32]{1,0:T(8,128)S(1)}, f32[32,32]{1,0:T(8,128)S(1)}, u32[]{:S(2)}, u32[]{:S(2)}) collective-permute-start(f32[32,32]{1,0:T(8,128)S(1)} %convolution_bitcast_fusion), channel_id=1, source_target_pairs={{0,4},{4,8},{8,12},{12,16},{16,20},{20,24},{24,28},{1,5},{5,9},{9,... | collective-permute-start | bytes 12296 | tf_op jit(solution)/shard_map/ppermute | solution.py:34
  146.6 31.0 %all-gather = f32[128,16]{1,0:T(8,128)S(1)} all-gather(f32[16,16]{1,0:T(8,128)S(1)} %fusion.55), channel_id=2, replica_groups=mesh['sub'=8,'sec'=4] {'sub'}, dimensions={0}, use_global_device_ids=true | all-gather | bytes 9216 | tf_op jit(solution)/shard_map/all_gather | solution.py:95
  183.4 4.6 %collective-permute-start.9 = (f32[32,16]{0,1:T(8,128)S(1)}, f32[32,16]{0,1:T(8,128)S(1)}, u32[]{:S(2)}, u32[]{:S(2)}) collective-permute-start(f32[32,16]{0,1:T(8,128)S(1)} %bitcast.120), channel_id=1, source_target_pairs={{0,4},{4,8},{8,12},{12,16},{16,20},{20,24},{24,28},{1,5},{5,9},{9,... | collective-permute-start | bytes 6152 | tf_op jit(solution)/shard_map/ppermute | solution.py:34
  189.5 30.5 %all-gather.1 = f32[128,16]{1,0:T(8,128)S(1)} all-gather(f32[16,16]{1,0:T(8,128)S(1)} %fusion.57), channel_id=3, replica_groups=mesh['sub'=8,'sec'=4] {'sub'}, dimensions={0}, use_global_device_ids=true | all-gather | bytes 9216 | tf_op jit(solution)/shard_map/all_gather | solution.py:95
  224.4 3.0 %fusion.22 = f32[16,3,32,128]{3,0,2,1:T(8,128)S(1)} fusion(f32[16,32,1,1]{1,0,3,2:T(8,128)S(1)} %convolution_bitcast_fusion.3, f32[32,3,40,136]{3,0,2,1:T(8,128)} %copy-done.1), kind=kOutput, calls=%fused_computation.31 | convolution fusion | flops 75694080 | bytes 2361344 | tf_op jit(solution)/shard_map/ak,acxy->kcxy/dot_general | solution.py:100
  (88 shorter events, 51.8 us)
Async XLA Ops:
  0.0 145.0 %collective-permute-start.7 = (f32[32,16]{0,1:T(8,128)}, f32[32,16]{0,1:T(8,128)S(1)}, u32[]{:S(2)}, u32[]{:S(2)}) collective-permute-start(f32[32,16]{0,1:T(8,128)} %param.15), channel_id=1, source_target_pairs={{0,4},{4,8},{8,12},{12,16},{16,20},{20,24},{24,28},{1,5},{5,9},{9,... | collective-permute-start | bytes 6152 | tf_op jit(solution)/shard_map/ppermute | solution.py:34
  4.9 140.0 %collective-permute-start.5 = (f32[32,16]{0,1:T(8,128)}, f32[32,16]{0,1:T(8,128)S(1)}, u32[]{:S(2)}, u32[]{:S(2)}) collective-permute-start(f32[32,16]{0,1:T(8,128)} %param.15), channel_id=1, source_target_pairs={{4,0},{8,4},{12,8},{16,12},{20,16},{24,20},{28,24},{5,1},{9,5},{13... | collective-permute-start | bytes 6152 | tf_op jit(solution)/shard_map/ppermute | solution.py:34
  7.4 6.8 %collective-permute-start = (bf16[100,4,128]{2,1,0:T(4,128)(2,1)S(1)}, bf16[100,4,128]{2,1,0:T(4,128)(2,1)S(1)}, u32[]{:S(2)}, u32[]{:S(2)}) collective-permute-start(bf16[100,4,128]{2,1,0:T(4,128)(2,1)S(1)} %get-tuple-element.15), channel_id=1, source_target_pairs={{0,4},{4,8},{8,12},{12,16},{16,20},{20,24},{24,28},{1,5},{5,9},{9,... | collective-permute-start | bytes 307208 | tf_op jit(solution)/shard_map/ppermute | solution.py:25
  11.9 7.0 %collective-permute-start.1 = (bf16[100,4,128]{2,1,0:T(4,128)(2,1)S(1)}, bf16[100,4,128]{2,1,0:T(4,128)(2,1)S(1)}, u32[]{:S(2)}, u32[]{:S(2)}) collective-permute-start(bf16[100,4,128]{2,1,0:T(4,128)(2,1)S(1)} %get-tuple-element.16), channel_id=1, source_target_pairs={{4,0},{8,4},{12,8},{16,12},{20,16},{24,20},{28,24},{5,1},{9,5},{13... | collective-permute-start | bytes 307208 | tf_op jit(solution)/shard_map/ppermute | solution.py:26
  20.6 8.2 %copy-start = (bf16[32,3,32,128]{3,2,1,0:T(8,128)(2,1)S(1)}, bf16[32,3,32,128]{3,2,1,0:T(8,128)(2,1)}, u32[]{:S(2)}) copy-start(bf16[32,3,32,128]{3,2,1,0:T(8,128)(2,1)} %param.11) | copy-start | bytes 2359300
  20.6 8.2 %copy-start.2 = (bf16[3,32,128]{2,1,0:T(8,128)(2,1)S(1)}, bf16[3,32,128]{2,1,0:T(8,128)(2,1)}, u32[]{:S(2)}) copy-start(bf16[3,32,128]{2,1,0:T(8,128)(2,1)} %param.12) | copy-start | bytes 73732
  20.6 8.2 %copy-start.3 = (bf16[32,128]{1,0:T(8,128)(2,1)S(1)}, bf16[32,128]{1,0:T(8,128)(2,1)}, u32[]{:S(2)}) copy-start(bf16[32,128]{1,0:T(8,128)(2,1)} %param.13) | copy-start | bytes 24580
  22.4 5.8 %collective-permute-start.3 = (bf16[100,40,4]{0,1,2:T(8,128)(2,1)S(1)}, bf16[100,40,4]{0,1,2:T(8,128)(2,1)S(1)}, u32[]{:S(2)}, u32[]{:S(2)}) collective-permute-start(bf16[100,40,4]{0,1,2:T(8,128)(2,1)S(1)} %copy.30), channel_id=1, source_target_pairs={{1,0},{2,1},{3,2},{5,4},{6,5},{7,6},{9,8},{10,9},{11,10},{13,12},{... | collective-permute-start | bytes 96008 | tf_op jit(solution)/shard_map/ppermute | solution.py:26
  23.7 3.9 %collective-permute-start.2 = (bf16[100,40,4]{0,1,2:T(8,128)(2,1)S(1)}, bf16[100,40,4]{0,1,2:T(8,128)(2,1)S(1)}, u32[]{:S(2)}, u32[]{:S(2)}) collective-permute-start(bf16[100,40,4]{0,1,2:T(8,128)(2,1)S(1)} %copy.29), channel_id=1, source_target_pairs={{0,1},{1,2},{2,3},{4,5},{5,6},{6,7},{8,9},{9,10},{10,11},{12,13},{... | collective-permute-start | bytes 96008 | tf_op jit(solution)/shard_map/ppermute | solution.py:25
  111.3 27.6 %copy-start.1 = (f32[32,3,40,136]{3,0,2,1:T(8,128)}, f32[32,3,40,136]{3,0,2,1:T(8,128)S(1)}, u32[]{:S(2)}) copy-start(f32[32,3,40,136]{3,0,2,1:T(8,128)S(1)} %get-tuple-element.8) | copy-start | bytes 6266884
  111.4 6.3 %copy-start.4 = (f32[32,16]{0,1:T(8,128)S(1)}, f32[32,16]{0,1:T(8,128)}, u32[]{:S(2)}) copy-start(f32[32,16]{0,1:T(8,128)} %param.15) | copy-start | bytes 6148
  116.4 22.6 %collective-permute-start.4 = (f32[32,3,8,136]{3,0,2,1:T(8,128)S(1)}, f32[32,3,8,136]{3,0,2,1:T(8,128)S(1)}, u32[]{:S(2)}, u32[]{:S(2)}) collective-permute-start(f32[32,3,8,136]{3,0,2,1:T(8,128)S(1)} %slice.109), channel_id=1, source_target_pairs={{4,0},{8,4},{12,8},{16,12},{20,16},{24,20},{28,24},{5,1},{9,5},{13... | collective-permute-start | bytes 1253384 | tf_op jit(solution)/shard_map/ppermute | solution.py:34
  139.8 6.5 %collective-permute-start.6 = (f32[32,32]{1,0:T(8,128)S(1)}, f32[32,32]{1,0:T(8,128)S(1)}, u32[]{:S(2)}, u32[]{:S(2)}) collective-permute-start(f32[32,32]{1,0:T(8,128)S(1)} %convolution_bitcast_fusion), channel_id=1, source_target_pairs={{0,4},{4,8},{8,12},{12,16},{16,20},{20,24},{24,28},{1,5},{5,9},{9,... | collective-permute-start | bytes 12296 | tf_op jit(solution)/shard_map/ppermute | solution.py:34
  181.9 6.0 %collective-permute-start.8 = (f32[32,16]{0,1:T(8,128)S(1)}, f32[32,16]{0,1:T(8,128)S(1)}, u32[]{:S(2)}, u32[]{:S(2)}) collective-permute-start(f32[32,16]{0,1:T(8,128)S(1)} %bitcast.119), channel_id=1, source_target_pairs={{4,0},{8,4},{12,8},{16,12},{20,16},{24,20},{28,24},{5,1},{9,5},{13... | collective-permute-start | bytes 6152 | tf_op jit(solution)/shard_map/ppermute | solution.py:34
  183.4 5.9 %collective-permute-start.9 = (f32[32,16]{0,1:T(8,128)S(1)}, f32[32,16]{0,1:T(8,128)S(1)}, u32[]{:S(2)}, u32[]{:S(2)}) collective-permute-start(f32[32,16]{0,1:T(8,128)S(1)} %bitcast.120), channel_id=1, source_target_pairs={{0,4},{4,8},{8,12},{12,16},{16,20},{20,24},{24,28},{1,5},{5,9},{9,... | collective-permute-start | bytes 6152 | tf_op jit(solution)/shard_map/ppermute | solution.py:34
